TPU v7x, 128 devices: a whole 4x4x4 slice. The times are simulated.
128 devices in a mesh: vessel: 8 (over z, core), tissue: 16 (over y, x).
Axes of the slice: x: 4, y: 4, z: 4, core: 2. Of those that a mesh axis runs over, the one named last changes fastest.
Arguments:
- tissue_start: float32 [3, 32, 128, 128], P(None, 'vessel', 'tissue'), may hold values from 0 to 1
- consumption: float32 [3, 32, 128, 128], P(None, 'vessel', 'tissue'), may hold values from 0.002 to 0.05
- inlet: float32 [3, 512], P(None, ('vessel', 'tissue')), may hold values from 0.5 to 2
- flow: float32 [512, 256], P(('vessel', 'tissue')), may hold values from 0.3 to 30
- permeability: float32 [3], replicated, may hold values from 0.3 to 3
- intersection_count: int32 [512, 16], P(('vessel', 'tissue')), may hold values from 64 to 128, as said below
- intersection_segment: int32 [512, 16, 128], P(('vessel', 'tissue')), may hold values from 0 to 255
- intersection_voxel: int32 [512, 16, 128], P(('vessel', 'tissue')), may hold values from 0 to 4095
- intersection_weight: float32 [512, 16, 128], P(('vessel', 'tissue')), may hold values from 0.1 to 1
- upstream: int32 [512], P(('vessel', 'tissue')), may hold values from 0 to 511
Outputs:
- tissue_field: float32 [3, 32, 128, 128], P(None, 'vessel', 'tissue')
- vessel_field: float32 [3, 512, 256], P(None, ('vessel', 'tissue'))
Inputs may be any that keep to these rules, and one draw needn't show every extreme that they name: `intersection_count`: every block has all 128 slots live toward at least one tissue brick of its vessel part, at most 128 toward any, and at least 64 toward every other.
All inputs are finite; a program needn't handle non-finite values.
Results may differ from a plain program's by a relative error of at most 0.0001.
Values sent between devices are 32-bit elements; how exact they have to be, the bound alone decides.
No kernel may reach another device: no remote copies, remote signals or barrier semaphores. Data moves between devices by JAX's collectives and lax.ppermute only.
A program may use at most 128 MiB of HBM per device.

v0:
```python
import jax
import jax.numpy as jnp
from jax import lax
from jax.sharding import PartitionSpec as P

SEG = 256
OUTER = 2
SWEEPS = 4
DIFFUSION = (1.0, 0.7, 0.7)


def with_halo(value, sides, width):
    for axis, dim in sides:
        size, length = (lax.axis_size(axis), value.shape[dim])
        up = [(i, (i + 1) % size) for i in range(size - 1)]
        down = [(j, i) for i, j in up]
        last = lax.slice_in_dim(value, length - width, length, axis=dim)
        first = lax.slice_in_dim(value, 0, width, axis=dim)
        before = lax.ppermute(last, axis, up)
        after = lax.ppermute(first, axis, down)
        value = jnp.concatenate([before, value, after], axis=dim)
    return value


def combine(earlier, later):
    return (earlier[0] * later[0], later[0] * earlier[1] + later[1])


def relax_sweep(tissue, source, consumption):
    padded = with_halo(tissue, (("vessel", 1), ("tissue", 2)), 1)
    padded = jnp.pad(padded, ((0, 0), (0, 0), (0, 0), (1, 1)))
    neighbours = padded[:, 2:, 1:-1, 1:-1] + padded[:, :-2, 1:-1, 1:-1]
    neighbours = neighbours + padded[:, 1:-1, 2:, 1:-1] + padded[:, 1:-1, :-2, 1:-1]
    neighbours = neighbours + padded[:, 1:-1, 1:-1, 2:] + padded[:, 1:-1, 1:-1, :-2]
    rates = jnp.array(DIFFUSION, jnp.float32)[:, None, None, None]
    produced = jnp.zeros_like(tissue).at[2].set(2.0 * consumption[1] * tissue[1])
    return (source + produced + rates * neighbours) / (6.0 * rates + consumption)


def solve_blocks(arranged, flat_weight, flat_segment, flow, inflow_rows, permeability):

    def solve_block(block_items):
        slot_values, weight, segment, speed, inflow_row = block_items
        onehot = (segment[:, None] == jnp.arange(SEG)[None, :]).astype(jnp.float32)
        weight_sum = jnp.dot(weight, onehot, precision=lax.Precision.HIGHEST)
        gathered = jnp.dot(slot_values * weight[None, :], onehot, precision=lax.Precision.HIGHEST)
        denominator = speed[None, :] + permeability[:, None] * weight_sum[None, :]
        decay_rate = speed[None, :] / denominator
        drive_term = permeability[:, None] * gathered / denominator
        drive_term = drive_term.at[:, 0].add(decay_rate[:, 0] * inflow_row)
        _, vessel = lax.associative_scan(combine, (decay_rate, drive_term), axis=1)
        at_slot = jnp.dot(vessel, onehot.T, precision=lax.Precision.HIGHEST)
        slot_flux = permeability[:, None] * weight[None, :] * (at_slot - slot_values)
        return (vessel, slot_flux)

    return lax.map(solve_block, (arranged, flat_weight, flat_segment, flow, inflow_rows))


def shards(
    tissue_start,
    consumption,
    inlet,
    flow,
    permeability,
    intersection_count,
    intersection_segment,
    intersection_voxel,
    intersection_weight,
    upstream,
):
    blocks_here, columns, slots = intersection_voxel.shape
    species, depth, rows_here, width = tissue_start.shape
    voxels = depth * rows_here * width
    live_slot = jnp.arange(slots)[None, None, :] < intersection_count[:, :, None]
    weight = jnp.where(live_slot, intersection_weight, 0.0)
    flat_weight = weight.reshape(blocks_here, -1)
    flat_segment = intersection_segment.reshape(blocks_here, -1)
    full_rows = rows_here * columns
    column = jnp.arange(columns)[None, :, None]
    region_index = (
        intersection_voxel // (rows_here * width) * full_rows
        + column * rows_here
        + intersection_voxel // width % rows_here
    ) * width + intersection_voxel % width
    region_index = region_index.reshape(-1)
    tissue = tissue_start
    inflow_rows = inlet.T
    vessel = jnp.zeros((blocks_here, species, SEG), jnp.float32)
    for outer_step in range(OUTER):
        region = lax.all_gather(tissue, "tissue", axis=2, tiled=True).reshape(species, -1)
        slot_values = region[:, region_index].reshape(species, blocks_here, columns, slots)
        arranged = jnp.swapaxes(slot_values, 0, 1).reshape(blocks_here, species, -1)
        vessel, slot_flux = solve_blocks(
            arranged, flat_weight, flat_segment, flow, inflow_rows, permeability
        )
        gathered_ends = lax.all_gather(
            vessel[:, :, SEG - 1], ("vessel", "tissue"), axis=0, tiled=True
        )
        inflow_rows = 0.5 * (inlet.T + gathered_ends[upstream])
        flux_grid = jnp.swapaxes(slot_flux.reshape(blocks_here, species, columns, slots), 0, 1)
        partial_source = jax.vmap(
            lambda species_row: jax.ops.segment_sum(species_row, region_index, voxels * columns)
        )(flux_grid.reshape(species, -1))
        source = lax.psum_scatter(
            partial_source.reshape(species, depth, full_rows, width),
            "tissue",
            scatter_dimension=2,
            tiled=True,
        )
        for sweep_step in range(SWEEPS):
            tissue = relax_sweep(tissue, source, consumption)
    return (tissue, jnp.swapaxes(vessel, 0, 1))


def solution(mesh):
    return jax.shard_map(
        shards,
        mesh=mesh,
        in_specs=(
            P(None, "vessel", "tissue", None),
            P(None, "vessel", "tissue", None),
            P(None, ("vessel", "tissue")),
            P(("vessel", "tissue"), None),
            P(),
            P(("vessel", "tissue"), None),
            P(("vessel", "tissue"), None, None),
            P(("vessel", "tissue"), None, None),
            P(("vessel", "tissue"), None, None),
            P(("vessel", "tissue")),
        ),
        out_specs=(P(None, "vessel", "tissue", None), P(None, ("vessel", "tissue"), None)),
        check_vma=False,
    )
```

profile of v0, /device:TPU:40, one launch (start us, length us, event | category | flops | bytes accessed | tf_op | source)
XLA Modules:
  0.0 754.9 jit_solution(14316864906050526464)
XLA Ops:
  7.2 25.3 %all_gather.9 = f32[3,4,128,128]{3,2,1,0:T(8,128)S(1)} all-gather(f32[3,4,8,128]{3,2,1,0:T(8,128)} %param.42), channel_id=1, replica_groups=mesh['vessel'=8,'tissue'=16] {'tissue'}, dimensions={2}, use_global_device_ids=true | all-gather | bytes 835584 | tf_op jit(solution)/shard_map/all_gather | solution.py:90
  32.5 16.6 %copy.52 = f32[3,4,128,128]{0,3,2,1:T(8,128)} copy(f32[3,4,128,128]{3,2,1,0:T(8,128)S(1)} %all_gather.9) | data formatting | bytes 1572864 | tf_op jit(solution)/shard_map/all_gather | solution.py:90
  49.3 38.3 %gather_fusion = f32[8192,3]{1,0:T(8,128)} fusion(f32[3,65536]{0,1:T(8,128)} %bitcast.162, s32[8192]{0:T(1024)S(1)} %broadcast_clamp_fusion), kind=kCustom, calls=%fused_computation | custom fusion | bytes 229376 | tf_op jit(solution)/shard_map/gather | solution.py:91
  87.6 2.8 copy.53
  90.8 48.8 %while.38 = (s32[]{:T(128)}, f32[4,3,256]{2,1,0:T(4,128)S(1)}, f32[4,3,2048]{2,1,0:T(4,128)S(1)}, f32[3]{0:T(128)S(1)}, f32[4,3,2048]{2,0,1:T(4,128)S(1)}, /*ind...) while((s32[]{:T(128)}, f32[4,3,256]{2,1,0:T(4,128)S(1)}, ...), condition=%wide.region_2.3_spmd, body=%wide.region_0.2_spmd.sunk | while | flops 45649856 | bytes 347579 | solution.py:56
  139.7 2.7 copy.68
  142.4 57.5 %scatter_custom_fusion = f32[3,65536]{0,1:T(8,128)} fusion(s32[8192]{0:T(1024)S(1)} %bitcast.196, f32[8192,3]{1,0:T(8,128)} %bitcast.167, f32[]{:T(128)} %constant.353.clone.1), kind=kCustom, calls=%fused_computation.111 | custom fusion | flops 24576 | bytes 786944 | tf_op jit(solution)/shard_map/vmap()/scatter-add | solution.py:102
  199.9 20.3 %copy.58 = f32[3,4,128,128]{3,2,1,0:T(8,128)} copy(f32[3,4,128,128]{0,3,2,1:T(8,128)} %bitcast.161) | data formatting | bytes 1572864 | tf_op jit(solution)/shard_map/reshape | solution.py:105
  222.2 3.6 collective-permute-start
  227.3 4.5 collective-permute-start.2
  233.7 5.8 collective-permute-done.3
  239.7 53.1 %reduce-scatter.3.cloned.1.call-done = f32[3,4,8,128]{3,2,1,0:T(8,128)} async-done(((f32[3,4,128,128]{3,2,1,0:T(8,128)}), f32[3,4,8,128]{3,2,1,0:T(8,128)}) %reduce-scatter.3.cloned.1.call-update) | async-done | bytes 49168 | tf_op jit(solution)/shard_map/reduce_scatter | solution.py:104
  299.4 2.4 collective-permute-start.5
  301.8 2.6 collective-permute-done.5
  304.4 4.6 collective-permute-start.6
  311.0 5.7 collective-permute-done.7
  318.9 2.4 collective-permute-start.9
  321.6 55.9 %all-gather = f32[512,3,1]{1,2,0:T(1,128)S(1)} all-gather(f32[4,3,1]{1,2,0:T(1,128)S(1)} %slice.1438), channel_id=2, replica_groups=mesh['vessel'=8,'tissue'=16] {'vessel','tissue'}, dimensions={0}, use_global_device_ids=true | all-gather | bytes 6192 | tf_op jit(solution)/shard_map/all_gather | solution.py:96
  378.1 3.4 collective-permute-start.10
  381.5 2.4 collective-permute-start.11
  384.0 5.2 collective-permute-done.11
  389.5 2.6 collective-permute-start.12
  394.1 4.2 collective-permute-done.13
  400.3 3.9 collective-permute-start.15
  404.2 3.7 collective-permute-done.15
  408.3 23.5 %all_gather.10 = f32[3,4,128,128]{3,2,1,0:T(8,128)S(1)} all-gather(f32[3,4,8,128]{3,2,1,0:T(8,128)S(1)} %fusion.65), channel_id=1, replica_groups=mesh['vessel'=8,'tissue'=16] {'tissue'}, dimensions={2}, use_global_device_ids=true | all-gather | bytes 835584 | tf_op jit(solution)/shard_map/all_gather | solution.py:90
  431.8 16.6 %copy.59 = f32[3,4,128,128]{0,3,2,1:T(8,128)} copy(f32[3,4,128,128]{3,2,1,0:T(8,128)S(1)} %all_gather.10) | data formatting | bytes 1572864 | tf_op jit(solution)/shard_map/all_gather | solution.py:90
  448.4 38.3 %gather_fusion.1 = f32[8192,3]{1,0:T(8,128)} fusion(f32[3,65536]{0,1:T(8,128)} %bitcast.163, s32[8192]{0:T(1024)S(1)} %broadcast_clamp_fusion), kind=kCustom, calls=%fused_computation.1 | custom fusion | bytes 229376 | tf_op jit(solution)/shard_map/gather | solution.py:91
  486.6 2.8 copy.60
  489.5 49.1 %while.39 = (s32[]{:T(128)}, f32[4,3,256]{2,0,1:T(4,128)S(1)}, f32[4,3,2048]{2,1,0:T(4,128)S(1)}, f32[3]{0:T(128)S(1)}, f32[4,3,2048]{2,0,1:T(4,128)S(1)}, /*ind...) while((s32[]{:T(128)}, f32[4,3,256]{2,0,1:T(4,128)S(1)}, ...), condition=%wide.region_7.8_spmd, body=%wide.region_5.7_spmd.sunk | while | flops 45649856 | bytes 356795 | solution.py:56
  538.8 2.7 copy.70
  541.5 57.5 %scatter_custom_fusion.1 = f32[3,65536]{0,1:T(8,128)} fusion(s32[8192]{0:T(1024)S(1)} %bitcast.197, f32[8192,3]{1,0:T(8,128)} %bitcast.166, f32[]{:T(128)} %constant.353.clone.1), kind=kCustom, calls=%fused_computation.109 | custom fusion | flops 24576 | bytes 786944 | tf_op jit(solution)/shard_map/vmap()/scatter-add | solution.py:102
  599.0 20.2 %copy.65 = f32[3,4,128,128]{3,2,1,0:T(8,128)} copy(f32[3,4,128,128]{0,3,2,1:T(8,128)} %bitcast.160) | data formatting | bytes 1572864 | tf_op jit(solution)/shard_map/reshape | solution.py:105
  621.1 2.4 collective-permute-start.17
  623.6 2.6 collective-permute-done.17
  626.2 4.6 collective-permute-start.18
  632.7 5.7 collective-permute-done.19
  638.7 50.8 %reduce-scatter.5.cloned.1.call-done = f32[3,4,8,128]{3,2,1,0:T(8,128)} async-done(((f32[3,4,128,128]{3,2,1,0:T(8,128)}), f32[3,4,8,128]{3,2,1,0:T(8,128)}) %reduce-scatter.5.cloned.1.call-update) | async-done | bytes 49168 | tf_op jit(solution)/shard_map/reduce_scatter | solution.py:104
  698.5 2.6 collective-permute-done.21
  701.1 4.6 collective-permute-start.22
  707.6 5.7 collective-permute-done.23
  715.6 2.4 collective-permute-start.25
  718.0 2.6 collective-permute-done.25
  722.6 3.9 collective-permute-start.27
  726.5 3.7 collective-permute-done.27
  734.9 2.6 collective-permute-done.29
  739.5 3.9 collective-permute-start.31
  743.4 3.7 collective-permute-done.31
  (920 shorter events, 145.0 us)
Async XLA Ops:
  7.2 285.7 %reduce-scatter.3.cloned.1.call-start = ((), (), s32[]{:S(2)}) async-start(), calls=%async_computation.2 | async-start | bytes 835584 | tf_op jit(solution)/shard_map/reduce_scatter | solution.py:104
  32.5 16.6 %copy-start.5 = (s32[4,16,128]{2,1,0:T(8,128)S(1)}, s32[4,16,128]{2,1,0:T(8,128)}, u32[]{:S(2)}) copy-start(s32[4,16,128]{2,1,0:T(8,128)} %param.49) | copy-start | bytes 98308
  49.1 41.3 %copy-start.6 = (f32[4,16,128]{2,1,0:T(8,128)S(1)}, f32[4,16,128]{2,1,0:T(8,128)}, u32[]{:S(2)}) copy-start(f32[4,16,128]{2,1,0:T(8,128)} %param.50) | copy-start | bytes 98308
  49.1 41.3 %copy-start.9 = (s32[4,16]{1,0:T(4,128)S(1)}, s32[4,16]{1,0:T(4,128)}, u32[]{:S(2)}) copy-start(s32[4,16]{1,0:T(4,128)} %param.47) | copy-start | bytes 772
  49.1 41.5 %copy-start.7 = (s32[4,16,128]{2,1,0:T(8,128)S(1)}, s32[4,16,128]{2,1,0:T(8,128)}, u32[]{:S(2)}) copy-start(s32[4,16,128]{2,1,0:T(8,128)} %param.48) | copy-start | bytes 98308
  49.1 41.5 %copy-start.10 = (f32[3,4]{1,0:T(4,128)S(1)}, f32[3,4]{1,0:T(4,128)}, u32[]{:S(2)}) copy-start(f32[3,4]{1,0:T(4,128)} %param.44) | copy-start | bytes 148
  49.2 41.6 %copy-start.2 = (f32[3]{0:T(128)S(1)}, f32[3]{0:T(128)}, u32[]{:S(2)}) copy-start(f32[3]{0:T(128)} %param.46) | copy-start | bytes 40
  49.2 41.6 %copy-start.8 = (f32[4,256]{1,0:T(4,128)S(1)}, f32[4,256]{1,0:T(4,128)}, u32[]{:S(2)}) copy-start(f32[4,256]{1,0:T(4,128)} %param.45) | copy-start | bytes 12292
  199.9 20.4 %copy-start.1 = (f32[3,4,8,128]{3,2,1,0:T(8,128)S(1)}, f32[3,4,8,128]{3,2,1,0:T(8,128)}, u32[]{:S(2)}) copy-start(f32[3,4,8,128]{3,2,1,0:T(8,128)} %param.42) | copy-start | bytes 147460
  199.9 95.3 %copy-start = (f32[3,4,8,128]{3,2,1,0:T(8,128)S(1)}, f32[3,4,8,128]{3,2,1,0:T(8,128)}, u32[]{:S(2)}) copy-start(f32[3,4,8,128]{3,2,1,0:T(8,128)} %param.43) | copy-start | bytes 147460
  199.9 96.6 %copy-start.3 = (f32[3]{0:T(128)S(1)}, f32[3]{0:T(128)}, u32[]{:S(2)}) copy-start(f32[3]{0:T(128)} %constant.459) | copy-start | bytes 40
  199.9 96.6 %copy-start.4 = (f32[3]{0:T(128)S(1)}, f32[3]{0:T(128)}, u32[]{:S(2)}) copy-start(f32[3]{0:T(128)} %constant.369.clone) | copy-start | bytes 40
  199.9 101.9 %copy-start.12 = (s32[4]{0:T(128)S(1)}, s32[4]{0:T(128)}, u32[]{:S(2)}) copy-start(s32[4]{0:T(128)} %param.51) | copy-start | bytes 52
  220.2 469.3 %reduce-scatter.5.cloned.1.call-start = ((), (), s32[]{:S(2)}) async-start(), calls=%async_computation.3 | async-start | bytes 835584 | tf_op jit(solution)/shard_map/reduce_scatter | solution.py:104
  220.3 5.6 collective-permute-start.1
  222.2 5.0 collective-permute-start
  227.3 6.4 collective-permute-start.2
  231.8 7.7 %collective-permute-start.3 = (f32[3,6,1,128]{3,2,1,0:T(1,128)S(1)}, f32[3,6,1,128]{3,2,1,0:T(1,128)S(1)}, u32[]{:S(2)}, u32[]{:S(2)}) collective-permute-start(f32[3,6,1,128]{3,2,1,0:T(1,128)S(1)} %get-tuple-element.476), channel_id=1, source_target_pairs={{0,1},{1,2},{2,3},{3,4},{4,5},{5,6},{6,7},{7,8},{8,9},{9,10},{10,1... | collective-permute-start | bytes 27656 | tf_op jit(solution)/shard_map/ppermute | solution.py:19
  297.5 4.4 collective-permute-start.4
  299.4 5.0 collective-permute-start.5
  304.4 6.5 collective-permute-start.6
  309.0 7.7 %collective-permute-start.7 = (f32[3,6,1,128]{3,2,1,0:T(1,128)S(1)}, f32[3,6,1,128]{3,2,1,0:T(1,128)S(1)}, u32[]{:S(2)}, u32[]{:S(2)}) collective-permute-start(f32[3,6,1,128]{3,2,1,0:T(1,128)S(1)} %get-tuple-element.474), channel_id=1, source_target_pairs={{0,1},{1,2},{2,3},{3,4},{4,5},{5,6},{6,7},{7,8},{8,9},{9,10},{10,1... | collective-permute-start | bytes 27656 | tf_op jit(solution)/shard_map/ppermute | solution.py:19
  317.0 61.0 %collective-permute-start.8 = (f32[3,1,8,128]{3,2,1,0:T(8,128)S(1)}, f32[3,1,8,128]{3,2,1,0:T(8,128)S(1)}, u32[]{:S(2)}, u32[]{:S(2)}) collective-permute-start(f32[3,1,8,128]{3,2,1,0:T(8,128)S(1)} %get-tuple-element.489), channel_id=1, source_target_pairs={{16,0},{32,16},{48,32},{64,48},{80,64},{96,80},{112,96},{17,1},{33... | collective-permute-start | bytes 36872 | tf_op jit(solution)/shard_map/ppermute | solution.py:20
  318.9 59.1 %collective-permute-start.9 = (f32[3,1,8,128]{3,2,1,0:T(8,128)S(1)}, f32[3,1,8,128]{3,2,1,0:T(8,128)S(1)}, u32[]{:S(2)}, u32[]{:S(2)}) collective-permute-start(f32[3,1,8,128]{3,2,1,0:T(8,128)S(1)} %get-tuple-element.488), channel_id=1, source_target_pairs={{0,16},{16,32},{32,48},{48,64},{64,80},{80,96},{96,112},{1,17},{17... | collective-permute-start | bytes 36872 | tf_op jit(solution)/shard_map/ppermute | solution.py:19
  378.1 5.9 collective-permute-start.10
  381.5 7.7 %collective-permute-start.11 = (f32[3,6,1,128]{3,2,1,0:T(1,128)S(1)}, f32[3,6,1,128]{3,2,1,0:T(1,128)S(1)}, u32[]{:S(2)}, u32[]{:S(2)}) collective-permute-start(f32[3,6,1,128]{3,2,1,0:T(1,128)S(1)} %get-tuple-element.472), channel_id=1, source_target_pairs={{0,1},{1,2},{2,3},{3,4},{4,5},{5,6},{6,7},{7,8},{8,9},{9,10},{10,1... | collective-permute-start | bytes 27656 | tf_op jit(solution)/shard_map/ppermute | solution.py:19
  389.5 4.6 collective-permute-start.12
  392.1 6.2 collective-permute-start.13
  398.3 5.9 collective-permute-start.14
  400.3 7.7 %collective-permute-start.15 = (f32[3,6,1,128]{3,2,1,0:T(1,128)S(1)}, f32[3,6,1,128]{3,2,1,0:T(1,128)S(1)}, u32[]{:S(2)}, u32[]{:S(2)}) collective-permute-start(f32[3,6,1,128]{3,2,1,0:T(1,128)S(1)} %get-tuple-element.470), channel_id=1, source_target_pairs={{0,1},{1,2},{2,3},{3,4},{4,5},{5,6},{6,7},{7,8},{8,9},{9,10},{10,1... | collective-permute-start | bytes 27656 | tf_op jit(solution)/shard_map/ppermute | solution.py:19
  538.7 60.3 %copy-start.11 = (f32[4,3,256]{2,0,1:T(4,128)}, f32[4,3,256]{2,0,1:T(4,128)S(1)}, u32[]{:S(2)}) copy-start(f32[4,3,256]{2,0,1:T(4,128)S(1)} %get-tuple-element.353) | copy-start | bytes 36868
  619.2 4.3 collective-permute-start.16
  621.1 5.0 collective-permute-start.17
  626.2 6.5 collective-permute-start.18
  630.8 7.7 %collective-permute-start.19 = (f32[3,6,1,128]{3,2,1,0:T(1,128)S(1)}, f32[3,6,1,128]{3,2,1,0:T(1,128)S(1)}, u32[]{:S(2)}, u32[]{:S(2)}) collective-permute-start(f32[3,6,1,128]{3,2,1,0:T(1,128)S(1)} %get-tuple-element.468), channel_id=1, source_target_pairs={{0,1},{1,2},{2,3},{3,4},{4,5},{5,6},{6,7},{7,8},{8,9},{9,10},{10,1... | collective-permute-start | bytes 27656 | tf_op jit(solution)/shard_map/ppermute | solution.py:19
  694.1 4.3 collective-permute-start.20
  696.0 5.0 collective-permute-start.21
  701.1 6.6 collective-permute-start.22
  705.7 7.7 %collective-permute-start.23 = (f32[3,6,1,128]{3,2,1,0:T(1,128)S(1)}, f32[3,6,1,128]{3,2,1,0:T(1,128)S(1)}, u32[]{:S(2)}, u32[]{:S(2)}) collective-permute-start(f32[3,6,1,128]{3,2,1,0:T(1,128)S(1)} %get-tuple-element.466), channel_id=1, source_target_pairs={{0,1},{1,2},{2,3},{3,4},{4,5},{5,6},{6,7},{7,8},{8,9},{9,10},{10,1... | collective-permute-start | bytes 27656 | tf_op jit(solution)/shard_map/ppermute | solution.py:19
  713.7 4.3 collective-permute-start.24
  715.6 5.0 collective-permute-start.25
  720.6 5.9 collective-permute-start.26
  722.6 7.7 %collective-permute-start.27 = (f32[3,6,1,128]{3,2,1,0:T(1,128)S(1)}, f32[3,6,1,128]{3,2,1,0:T(1,128)S(1)}, u32[]{:S(2)}, u32[]{:S(2)}) collective-permute-start(f32[3,6,1,128]{3,2,1,0:T(1,128)S(1)} %get-tuple-element.464), channel_id=1, source_target_pairs={{0,1},{1,2},{2,3},{3,4},{4,5},{5,6},{6,7},{7,8},{8,9},{9,10},{10,1... | collective-permute-start | bytes 27656 | tf_op jit(solution)/shard_map/ppermute | solution.py:19
  730.6 4.3 collective-permute-start.28
  732.5 5.0 collective-permute-start.29
  737.5 5.9 collective-permute-start.30
  739.5 7.7 %collective-permute-start.31 = (f32[3,6,1,128]{3,2,1,0:T(1,128)S(1)}, f32[3,6,1,128]{3,2,1,0:T(1,128)S(1)}, u32[]{:S(2)}, u32[]{:S(2)}) collective-permute-start(f32[3,6,1,128]{3,2,1,0:T(1,128)S(1)} %get-tuple-element.462), channel_id=1, source_target_pairs={{0,1},{1,2},{2,3},{3,4},{4,5},{5,6},{6,7},{7,8},{8,9},{9,10},{10,1... | collective-permute-start | bytes 27656 | tf_op jit(solution)/shard_map/ppermute | solution.py:19
Sparse Core Ops, SparseCore 0:
  220.3 72.4 reduce-scatter.2
  619.3 70.1 reduce-scatter.4
where the time goes:
time: 757 us; the launch traced here: 755 us
  local copies, waits for them, and re-layouts  224 us (30%)
  waiting for transfers between devices  162 us (21%)
  other arithmetic  141 us (19%)
  blocking collectives  105 us (14%)
  starting transfers between devices  85.4 us (11%)
  matrix products  21.3 us (3%)
  between operations  14.9 us (2%)
    scatter-add x2, other arithmetic, shards(): jax.ops.segment_sum(species_row, region_index, voxels * columns)  115 us
    reduce_scatter x2, waiting for transfers between devices, shards(): lax.psum_scatter(partial_source.reshape(species, depth, full_rows, width)...  104 us
    gather x2, local copies, waits for them, and re-layouts, shards(): region[:, region_index].reshape(species, blocks_here, columns, slots)  76.5 us
    ppermute x16, waiting for transfers between devices, with_halo(): before = lax.ppermute(last, axis, up)  56.4 us
    all_gather x1, blocking collectives, shards(): lax.all_gather(vessel[:, :, SEG - 1], ('vessel', 'tissue'), axis=0, tiled...  55.9 us
    all_gather x2, blocking collectives, shards(): lax.all_gather(tissue, 'tissue', axis=2, tiled=True).reshape(species, -1)  48.8 us
    ppermute x16, starting transfers between devices, with_halo(): after = lax.ppermute(first, axis, down)  45.2 us
    slice x320, local copies, waits for them, and re-layouts, solve_block(): _, vessel = lax.associative_scan(combine, (decay_rate, drive_term), axis=1)  41.6 us
  transfers between devices with their start and end apart: 34, of which 17 were waited for; matrix products, arithmetic and copies ran while one was open for 0% of the time, Pallas kernels for 0%

commit v1 on v0

--- a/solution.py
+++ b/solution.py
@@ -1,3 +1,4 @@
+import functools
 import jax
 import jax.numpy as jnp
 from jax import lax
@@ -7,6 +8,34 @@
 OUTER = 2
 SWEEPS = 4
 DIFFUSION = (1.0, 0.7, 0.7)
+
+
+def manage_row(load, mesh_dim, row_dim):
+    y2 = jax.lax.axis_size(mesh_dim)
+    x_next = jax.lax.axis_index(mesh_dim)
+    r_now, low, v_next = (y2, x_next, load.shape[row_dim])
+    seen = tuple(((j0, (j0 + 1) % r_now) for j0 in range(r_now)))
+    panels = tuple(((j0, (j0 - 1) % r_now) for j0 in range(r_now)))
+    tile_out = jnp.zeros(
+        (*load.shape[:row_dim], r_now * v_next, *load.shape[row_dim + 1 :]), load.dtype
+    )
+    tile_out = lax.dynamic_update_slice_in_dim(tile_out, load, low * v_next, axis=row_dim)
+    res = block_now = load
+    f_next = r_now // 2
+    for dev_i in range(1, f_next + 1):
+        res = jax.lax.ppermute(res, mesh_dim, seen)
+        tile_out = lax.dynamic_update_slice_in_dim(
+            tile_out, res, (low - dev_i) % r_now * v_next, axis=row_dim
+        )
+        if dev_i < r_now - f_next:
+            block_now = jax.lax.ppermute(block_now, mesh_dim, panels)
+            tile_out = lax.dynamic_update_slice_in_dim(
+                tile_out, block_now, (low + dev_i) % r_now * v_next, axis=row_dim
+            )
+    return tile_out
+
+
+process_the_patch = functools.partial(manage_row, mesh_dim="tissue", row_dim=2)
 
 
 def with_halo(value, sides, width):
@@ -87,7 +116,7 @@
     inflow_rows = inlet.T
     vessel = jnp.zeros((blocks_here, species, SEG), jnp.float32)
     for outer_step in range(OUTER):
-        region = lax.all_gather(tissue, "tissue", axis=2, tiled=True).reshape(species, -1)
+        region = process_the_patch(tissue).reshape(species, -1)
         slot_values = region[:, region_index].reshape(species, blocks_here, columns, slots)
         arranged = jnp.swapaxes(slot_values, 0, 1).reshape(blocks_here, species, -1)
         vessel, slot_flux = solve_blocks(

time: 757 us -> 865 us (1.14)
  local copies, waits for them, and re-layouts: 224 us -> 283 us
  starting transfers between devices: 85.4 us -> 143 us
  blocking collectives: 105 us -> 55.9 us
  waiting for transfers between devices: 162 us -> 178 us
  other arithmetic: 141 us -> 155 us
    ppermute x0 -> x30, starting transfers between devices: none -> 58.6 us  [the longest x14 56.4 us: manage_row(): block_now = jax.lax.ppermute(block_now, mesh_dim, panels)]
    dynamic_update_slice x0 -> x32, local copies, waits for them, and re-layouts: none -> 49 us  [the longest x16 24.5 us: manage_row(): lax.dynamic_update_slice_in_dim(tile_out, res, (low - dev_i) % r_now * v_...]
    all_gather x2 -> x0, blocking collectives: 48.8 us -> none  [shards(): lax.all_gather(tissue, 'tissue', axis=2, tiled=True).reshape(species, -1)]
    all_gather x2 -> x0, local copies, waits for them, and re-layouts: 33.2 us -> none  [shards(): lax.all_gather(tissue, 'tissue', axis=2, tiled=True).reshape(species, -1)]
    another operation x2 -> x4, local copies, waits for them, and re-layouts: 0.04 us -> 22.6 us
    ppermute x0 -> x30, local copies, waits for them, and re-layouts: none -> 19 us  [the longest x16 10.1 us: manage_row(): res = jax.lax.ppermute(res, mesh_dim, seen)]
    scatter-add x2, other arithmetic: 115 us -> 128 us  [shards(): jax.ops.segment_sum(species_row, region_index, voxels * columns)]
    reduce_scatter x2, waiting for transfers between devices: 104 us -> 116 us  [shards(): lax.psum_scatter(partial_source.reshape(species, depth, full_rows, width)...]
  transfers between devices with their start and end apart: 34 -> 64, of which waited for: 17 -> 20; matrix products, arithmetic and copies ran while one was open for 0% -> 11% of each run, Pallas kernels for 0% -> 0%
where the time goes in v1:
time: 865 us; the launch traced here: 854 us
  local copies, waits for them, and re-layouts  283 us (33%)
  waiting for transfers between devices  178 us (21%)
  other arithmetic  155 us (18%)
  starting transfers between devices  143 us (17%)
  blocking collectives  55.9 us (6%)
  matrix products  21.3 us (2%)
  between operations  15.7 us (2%)
    scatter-add x2, other arithmetic, shards(): jax.ops.segment_sum(species_row, region_index, voxels * columns)  128 us
    reduce_scatter x2, waiting for transfers between devices, shards(): lax.psum_scatter(partial_source.reshape(species, depth, full_rows, width)...  116 us
    gather x2, local copies, waits for them, and re-layouts, shards(): region[:, region_index].reshape(species, blocks_here, columns, slots)  76.8 us
    ppermute x14, starting transfers between devices, manage_row(): block_now = jax.lax.ppermute(block_now, mesh_dim, panels)  56.4 us
    all_gather x1, blocking collectives, shards(): lax.all_gather(vessel[:, :, SEG - 1], ('vessel', 'tissue'), axis=0, tiled...  55.9 us
    ppermute x16, waiting for transfers between devices, with_halo(): before = lax.ppermute(last, axis, up)  52.6 us
    ppermute x16, starting transfers between devices, with_halo(): before = lax.ppermute(last, axis, up)  44 us
    slice x320, local copies, waits for them, and re-layouts, solve_block(): _, vessel = lax.associative_scan(combine, (decay_rate, drive_term), axis=1)  41.4 us
  transfers between devices with their start and end apart: 64, of which 20 were waited for; matrix products, arithmetic and copies ran while one was open for 11% of the time, Pallas kernels for 0%

profile of v1, /device:TPU:40, one launch (start us, length us, event | category | flops | bytes accessed | tf_op | source)
XLA Modules:
  0.0 854.3 jit_solution(14692155719659073340)
XLA Ops:
  14.6 11.3 %broadcast.401.clone = f32[3,4,128,128]{0,3,2,1:T(8,128)} broadcast(f32[]{:T(128)} %constant.468.clone.1), dimensions={} | broadcast | bytes 786436 | tf_op jit(solution)/shard_map/broadcast.27
  31.8 4.1 collective-permute-start.3
  40.2 4.1 collective-permute-start.5
  48.6 4.2 collective-permute-start.7
  57.1 4.1 collective-permute-start.9
  65.5 4.1 collective-permute-start.11
  74.1 4.2 collective-permute-start.13
  82.5 4.1 collective-permute-done.14
  88.7 38.4 %gather_fusion = f32[8192,3]{1,0:T(8,128)} fusion(f32[3,65536]{0,1:T(8,128)} %bitcast.19, s32[8192]{0:T(1024)S(1)} %broadcast_clamp_fusion), kind=kCustom, calls=%fused_computation | custom fusion | bytes 229376 | tf_op jit(solution)/shard_map/gather | solution.py:120
  127.1 2.8 copy.128
  130.1 48.8 %while.38 = (s32[]{:T(128)}, f32[4,3,256]{2,1,0:T(4,128)S(1)}, f32[4,3,2048]{2,1,0:T(4,128)S(1)}, f32[3]{0:T(128)S(1)}, f32[4,3,2048]{2,0,1:T(4,128)S(1)}, /*ind...) while((s32[]{:T(128)}, f32[4,3,256]{2,1,0:T(4,128)S(1)}, ...), condition=%wide.region_2.3_spmd, body=%wide.region_0.2_spmd.sunk | while | flops 45649856 | bytes 347571 | solution.py:85
  181.6 70.0 %scatter_custom_fusion = f32[3,65536]{0,1:T(8,128)} fusion(s32[8192]{0:T(1024)S(1)} %bitcast.194, f32[8192,3]{1,0:T(8,128)} %bitcast.165, f32[]{:T(128)} %constant.468.clone.1), kind=kCustom, calls=%fused_computation.111 | custom fusion | flops 24576 | bytes 786944 | tf_op jit(solution)/shard_map/vmap()/scatter-add | solution.py:131
  251.7 20.2 %copy.133 = f32[3,4,128,128]{3,2,1,0:T(8,128)} copy(f32[3,4,128,128]{0,3,2,1:T(8,128)} %bitcast.161) | data formatting | bytes 1572864 | tf_op jit(solution)/shard_map/reshape | solution.py:134
  273.9 3.6 collective-permute-start.15
  281.0 3.9 collective-permute-start.18
  284.8 3.8 collective-permute-done.18
  288.9 62.1 %reduce-scatter.3.cloned.1.call-done = f32[3,4,8,128]{3,2,1,0:T(8,128)} async-done(((f32[3,4,128,128]{3,2,1,0:T(8,128)}), f32[3,4,8,128]{3,2,1,0:T(8,128)}) %reduce-scatter.3.cloned.1.call-update) | async-done | bytes 49168 | tf_op jit(solution)/shard_map/reduce_scatter | solution.py:133
  362.6 4.6 collective-permute-start.21
  369.1 5.7 collective-permute-done.22
  379.8 55.9 %all-gather = f32[512,3,1]{1,2,0:T(1,128)S(1)} all-gather(f32[4,3,1]{1,2,0:T(1,128)S(1)} %slice.1438), channel_id=2, replica_groups=mesh['vessel'=8,'tissue'=16] {'vessel','tissue'}, dimensions={0}, use_global_device_ids=true | all-gather | bytes 6192 | tf_op jit(solution)/shard_map/all_gather | solution.py:125
  436.2 3.4 collective-permute-start.25
  442.1 5.2 collective-permute-done.26
  452.2 4.2 collective-permute-done.28
  458.4 3.9 collective-permute-start.30
  462.4 3.7 collective-permute-done.30
  467.1 4.1 collective-permute-start.32
  471.3 11.3 %broadcast.401 = f32[3,4,128,128]{0,3,2,1:T(8,128)} broadcast(f32[]{:T(128)} %constant.468.clone.1), dimensions={} | broadcast | bytes 786436 | tf_op jit(solution)/shard_map/broadcast.27
  488.5 4.1 collective-permute-start.34
  497.1 4.1 collective-permute-start.36
  505.6 4.2 collective-permute-start.38
  514.3 4.1 collective-permute-start.40
  522.9 4.2 collective-permute-start.42
  531.7 4.2 collective-permute-start.44
  540.5 4.0 collective-permute-done.45
  546.7 38.4 %gather_fusion.1 = f32[8192,3]{1,0:T(8,128)} fusion(f32[3,65536]{0,1:T(8,128)} %bitcast.30, s32[8192]{0:T(1024)S(1)} %broadcast_clamp_fusion), kind=kCustom, calls=%fused_computation.1 | custom fusion | bytes 229376 | tf_op jit(solution)/shard_map/gather | solution.py:120
  585.1 2.8 copy.150
  588.0 49.1 %while.39 = (s32[]{:T(128)}, f32[4,3,256]{2,0,1:T(4,128)S(1)}, f32[4,3,2048]{2,1,0:T(4,128)S(1)}, f32[3]{0:T(128)S(1)}, f32[4,3,2048]{2,0,1:T(4,128)S(1)}, /*ind...) while((s32[]{:T(128)}, f32[4,3,256]{2,0,1:T(4,128)S(1)}, ...), condition=%wide.region_7.8_spmd, body=%wide.region_5.7_spmd.sunk | while | flops 45649856 | bytes 356787 | solution.py:85
  639.9 57.7 %scatter_custom_fusion.1 = f32[3,65536]{0,1:T(8,128)} fusion(s32[8192]{0:T(1024)S(1)} %bitcast.195, f32[8192,3]{1,0:T(8,128)} %bitcast.164, f32[]{:T(128)} %constant.468.clone.1), kind=kCustom, calls=%fused_computation.109 | custom fusion | flops 24576 | bytes 786944 | tf_op jit(solution)/shard_map/vmap()/scatter-add | solution.py:131
  697.6 20.2 %copy.155 = f32[3,4,128,128]{3,2,1,0:T(8,128)} copy(f32[3,4,128,128]{0,3,2,1:T(8,128)} %bitcast.160) | data formatting | bytes 1572864 | tf_op jit(solution)/shard_map/reshape | solution.py:134
  726.9 3.8 collective-permute-start.49
  730.7 3.9 collective-permute-done.49
  734.8 53.7 %reduce-scatter.5.cloned.1.call-done = f32[3,4,8,128]{3,2,1,0:T(8,128)} async-done(((f32[3,4,128,128]{3,2,1,0:T(8,128)}), f32[3,4,8,128]{3,2,1,0:T(8,128)}) %reduce-scatter.5.cloned.1.call-update) | async-done | bytes 49168 | tf_op jit(solution)/shard_map/reduce_scatter | solution.py:133
  800.1 4.6 collective-permute-start.52
  806.6 5.7 collective-permute-done.53
  821.6 3.9 collective-permute-start.57
  825.5 3.7 collective-permute-done.57
  838.5 3.9 collective-permute-start.61
  842.4 3.7 collective-permute-done.61
  (1036 shorter events, 254.8 us)
Async XLA Ops:
  7.2 343.8 %reduce-scatter.3.cloned.1.call-start = ((), (), s32[]{:S(2)}) async-start(), calls=%async_computation.2 | async-start | bytes 835584 | tf_op jit(solution)/shard_map/reduce_scatter | solution.py:133
  7.2 20.3 %collective-permute-start = (f32[3,4,8,128]{3,2,1,0:T(8,128)}, f32[3,4,8,128]{3,2,1,0:T(8,128)S(1)}, u32[]{:S(2)}, u32[]{:S(2)}) collective-permute-start(f32[3,4,8,128]{3,2,1,0:T(8,128)} %param.42), channel_id=1, source_target_pairs={{0,1},{1,2},{2,3},{3,4},{4,5},{5,6},{6,7},{7,8},{8,9},{9,10},{10,1... | collective-permute-start | bytes 147464 | tf_op jit(solution)/shard_map/ppermute | solution.py:26
  8.8 20.9 %collective-permute-start.1 = (f32[3,4,8,128]{3,2,1,0:T(8,128)}, f32[3,4,8,128]{3,2,1,0:T(8,128)S(1)}, u32[]{:S(2)}, u32[]{:S(2)}) collective-permute-start(f32[3,4,8,128]{3,2,1,0:T(8,128)} %param.42), channel_id=1, source_target_pairs={{0,15},{1,0},{2,1},{3,2},{4,3},{5,4},{6,5},{7,6},{8,7},{9,8},{10,9... | collective-permute-start | bytes 147464 | tf_op jit(solution)/shard_map/ppermute | solution.py:31
  29.7 6.2 collective-permute-start.2
  31.8 6.2 collective-permute-start.3
  38.1 6.3 collective-permute-start.4
  40.2 6.3 collective-permute-start.5
  46.5 6.3 collective-permute-start.6
  48.6 6.4 collective-permute-start.7
  55.0 6.2 collective-permute-start.8
  57.1 6.2 collective-permute-start.9
  63.3 6.3 collective-permute-start.10
  65.5 6.5 collective-permute-start.11
  71.7 6.6 collective-permute-start.12
  74.1 6.3 collective-permute-start.13
  80.4 6.2 collective-permute-start.14
  271.9 516.6 %reduce-scatter.5.cloned.1.call-start = ((), (), s32[]{:S(2)}) async-start(), calls=%async_computation.3 | async-start | bytes 835584 | tf_op jit(solution)/shard_map/reduce_scatter | solution.py:133
  281.0 7.7 collective-permute-start.18
  362.6 6.5 collective-permute-start.21
  367.2 7.7 collective-permute-start.22
  375.2 61.0 %collective-permute-start.23 = (f32[3,1,8,128]{3,2,1,0:T(8,128)S(1)}, f32[3,1,8,128]{3,2,1,0:T(8,128)S(1)}, u32[]{:S(2)}, u32[]{:S(2)}) collective-permute-start(f32[3,1,8,128]{3,2,1,0:T(8,128)S(1)} %get-tuple-element.489), channel_id=1, source_target_pairs={{16,0},{32,16},{48,32},{64,48},{80,64},{96,80},{112,96},{17,1},{33... | collective-permute-start | bytes 36872 | tf_op jit(solution)/shard_map/ppermute | solution.py:49
  377.1 59.1 %collective-permute-start.24 = (f32[3,1,8,128]{3,2,1,0:T(8,128)S(1)}, f32[3,1,8,128]{3,2,1,0:T(8,128)S(1)}, u32[]{:S(2)}, u32[]{:S(2)}) collective-permute-start(f32[3,1,8,128]{3,2,1,0:T(8,128)S(1)} %get-tuple-element.488), channel_id=1, source_target_pairs={{0,16},{16,32},{32,48},{48,64},{64,80},{80,96},{96,112},{1,17},{17... | collective-permute-start | bytes 36872 | tf_op jit(solution)/shard_map/ppermute | solution.py:48
  436.2 5.9 collective-permute-start.25
  439.6 7.7 collective-permute-start.26
  450.3 6.2 collective-permute-start.28
  456.5 5.9 collective-permute-start.29
  458.4 7.7 collective-permute-start.30
  467.0 17.0 %collective-permute-start.31 = (f32[3,4,8,128]{3,2,1,0:T(8,128)S(1)}, f32[3,4,8,128]{3,2,1,0:T(8,128)S(1)}, u32[]{:S(2)}, u32[]{:S(2)}) collective-permute-start(f32[3,4,8,128]{3,2,1,0:T(8,128)S(1)} %fusion.65), channel_id=1, source_target_pairs={{0,1},{1,2},{2,3},{3,4},{4,5},{5,6},{6,7},{7,8},{8,9},{9,10},{10,1... | collective-permute-start | bytes 147464 | tf_op jit(solution)/shard_map/ppermute | solution.py:26
  467.1 19.2 %collective-permute-start.32 = (f32[3,4,8,128]{3,2,1,0:T(8,128)S(1)}, f32[3,4,8,128]{3,2,1,0:T(8,128)S(1)}, u32[]{:S(2)}, u32[]{:S(2)}) collective-permute-start(f32[3,4,8,128]{3,2,1,0:T(8,128)S(1)} %fusion.65), channel_id=1, source_target_pairs={{0,15},{1,0},{2,1},{3,2},{4,3},{5,4},{6,5},{7,6},{8,7},{9,8},{10,9... | collective-permute-start | bytes 147464 | tf_op jit(solution)/shard_map/ppermute | solution.py:31
  486.3 6.3 collective-permute-start.33
  488.5 6.3 collective-permute-start.34
  494.8 6.4 collective-permute-start.35
  497.1 6.4 collective-permute-start.36
  503.4 6.4 collective-permute-start.37
  505.6 6.4 collective-permute-start.38
  512.1 6.3 collective-permute-start.39
  514.3 6.3 collective-permute-start.40
  520.6 6.7 collective-permute-start.41
  522.9 6.7 collective-permute-start.42
  529.5 6.4 collective-permute-start.43
  531.7 6.6 collective-permute-start.44
  538.1 6.4 collective-permute-start.45
  726.9 7.7 collective-permute-start.49
  800.1 6.5 collective-permute-start.52
  804.7 7.7 collective-permute-start.53
  819.6 5.9 collective-permute-start.56
  821.6 7.7 collective-permute-start.57
  838.5 7.7 collective-permute-start.61
  (26 other events, 1153.4 us)
Sparse Core Ops, SparseCore 0:
  272.0 78.9 reduce-scatter.2
  717.9 70.5 reduce-scatter.4
